TPU v7x, 32 devices: a whole 2x2x4 slice. The times are simulated.
32 devices in a mesh: dev: 32 (over z, y, x, core).
Axes of the slice: x: 2, y: 2, z: 4, core: 2. Of those that a mesh axis runs over, the one named last changes fastest.
Arguments:
- inputs: bfloat16 [65536, 227], P('dev'), may hold values from -6 to 6
- targets: float32 [65536, 227], P('dev'), may hold values from -6 to 6
- geometry: bfloat16 [8192, 4], P('dev'), may hold values from -6 to 6
- land_sea: int32 [65536], P('dev'), may hold values 0 or 1
- level_mask: int32 [65536, 227], P('dev'), may hold values from 0 to 1
- edge_owners: int32 [8192, 2], P('dev'), may hold values from 0 to 31, all different within a row; in each aligned block of 256 rows (0 to 255, 256 to 511, ...) at most 20 rows name the same one
- edge_local: int32 [8192, 2], P('dev'), may hold values from 0 to 2047
- step_count: int32 [1], replicated, may hold values from 1 to 20
- master: float32 [6545408], P('dev'), as said below
- first_moment: float32 [6545408], P('dev'), as said below
- second_moment: float32 [6545408], P('dev'), as said below
- ema: float32 [6545408], P('dev'), as said below
Outputs:
- new_master: float32 [6545408], P('dev')
- new_first: float32 [6545408], P('dev')
- new_second: float32 [6545408], P('dev')
- new_ema: float32 [6545408], P('dev')
- loss: float32 [], replicated
- grad_norm: float32 [], replicated
Inputs may be any that keep to these rules, and one draw needn't show every extreme that they name: `edge_owners`: the two columns of a row differ; within the rows of one device no device is named more than 20 times, and some device is named exactly 20 times. `master`: Finite, of the size of fan-in scaled weights, gains near 1. `first_moment`: Finite, both signs. `second_moment`: Positive. `ema`: Finite, of the size of fan-in scaled weights, gains near 1.
All inputs are finite; a program needn't handle non-finite values. No bound on the sum of `land_sea` on one device may be relied on, other than what follows from the above.
Results may differ from a plain program's by a relative error of at most 0.00045.
The roundings to bfloat16 on the way count: a program that leaves them out, or rounds other values in their place, can miss the bound.
Values may be sent and summed in bfloat16 or wider, within the bound.
A program may use at most 192 MiB of HBM per device.

v0:
```python
import jax
import jax.numpy as jnp
import numpy as np
from jax import lax
from jax.sharding import PartitionSpec as P

LATENT = 512
VARS = 227
GEO = 4
SEA_VARS = 4
LAYERS = 3
PARAMS = 6545408
norm_eps = 1e-05
clip_limit = 0.01
beta_one = 0.9
beta_two = 0.999
adam_eps = 1e-08
learn_rate = 0.03
decay_rate = 0.1
ema_keep = 0.9


def layout(width, variables, geometry, layers):
    shapes = [(variables, width, True), (geometry, width, True)]
    for k in range(layers):
        shapes.append((3 * width, width, True))
        shapes.append((2 * width, width, True))
    shapes.append((width, variables, False))
    segments = []
    offset = 0
    for block_id, (fan_in, fan_out, normed) in enumerate(shapes):
        members = [
            ("w_in", (fan_in, width)),
            ("b_in", (width,)),
            ("w_out", (width, fan_out)),
            ("b_out", (fan_out,)),
        ]
        if normed:
            members = members + [("gain", (fan_out,)), ("shift", (fan_out,))]
        for part_name, part_shape in members:
            entries = int(np.prod(part_shape))
            segments.append((block_id, part_name, part_shape, offset, entries))
            offset += entries
    return (segments, offset)


def unpack(flat, segments):
    blocks = [dict() for k in range(segments[-1][0] + 1)]
    for block_id, part_name, part_shape, offset, entries in segments:
        blocks[block_id][part_name] = flat[offset : offset + entries].reshape(part_shape)
    return blocks


def mlp_forward(params, source):
    pre = jnp.dot(source, params["w_in"], preferred_element_type=jnp.float32) + params[
        "b_in"
    ].astype(jnp.float32)
    act = jax.nn.silu(pre).astype(jnp.bfloat16)
    post = jnp.dot(act, params["w_out"], preferred_element_type=jnp.float32) + params[
        "b_out"
    ].astype(jnp.float32)
    if "gain" in params:
        centred = post - jnp.mean(post, axis=-1, keepdims=True)
        inv_std = lax.rsqrt(jnp.mean(centred * centred, axis=-1, keepdims=True) + norm_eps)
        scaled = centred * inv_std
        result = scaled * params["gain"].astype(jnp.float32) + params["shift"].astype(jnp.float32)
        return (result, (source, pre, act, scaled, inv_std))
    return (post, (source, pre, act, None, None))


def mlp_backward(params, kept, grad_out, need_input):
    source, pre, act, scaled, inv_std = kept
    grads = {}
    if scaled is not None:
        grads["gain"] = jnp.sum(grad_out * scaled, axis=0)
        grads["shift"] = jnp.sum(grad_out, axis=0)
        grad_scaled = grad_out * params["gain"].astype(jnp.float32)
        grad_post = inv_std * (
            grad_scaled
            - jnp.mean(grad_scaled, axis=-1, keepdims=True)
            - scaled * jnp.mean(grad_scaled * scaled, axis=-1, keepdims=True)
        )
    else:
        grad_post = grad_out
    post_low = grad_post.astype(jnp.bfloat16)
    grads["w_out"] = jnp.einsum("ni,nj->ij", act, post_low, preferred_element_type=jnp.float32)
    grads["b_out"] = jnp.sum(post_low.astype(jnp.float32), axis=0)
    grad_act = jnp.einsum(
        "nj,ij->ni", post_low, params["w_out"], preferred_element_type=jnp.float32
    )
    sigma = jax.nn.sigmoid(pre)
    pre_low = (grad_act * sigma * (1.0 + pre * (1.0 - sigma))).astype(jnp.bfloat16)
    grads["w_in"] = jnp.einsum("ni,nj->ij", source, pre_low, preferred_element_type=jnp.float32)
    grads["b_in"] = jnp.sum(pre_low.astype(jnp.float32), axis=0)
    grad_source = None
    if need_input:
        grad_source = jnp.einsum(
            "nj,ij->ni", pre_low, params["w_in"], preferred_element_type=jnp.float32
        )
    return (grad_source, grads)


def make_routes(edge_owners, edge_local):
    devices = lax.axis_size("dev")
    edges_here = edge_owners.shape[0]
    capacity = 5 * edges_here // (2 * devices)
    wanted_owner = edge_owners.reshape(-1)
    wanted_local = edge_local.reshape(-1)
    one_hot = (wanted_owner[:, None] == jnp.arange(devices, dtype=jnp.int32)[None, :]).astype(
        jnp.int32
    )
    ranking = jnp.sum((jnp.cumsum(one_hot, axis=0) - 1) * one_hot, axis=1)
    position = wanted_owner * capacity + ranking
    asking = jnp.zeros((devices * capacity,), jnp.int32).at[position].set(wanted_local + 1)
    served = lax.all_to_all(
        asking.reshape(devices, capacity), "dev", split_axis=0, concat_axis=0, tiled=True
    ).reshape(-1)
    valid = served > 0
    served_rows = jnp.maximum(served - 1, 0)
    return (served_rows, valid, position, position[1::2], devices, capacity)


def layer_forward(edge_params, node_params, node, edge, routes):
    served_rows, valid, position, recv_pos, devices, capacity = routes
    node_low = node.astype(jnp.bfloat16)
    outgoing = jnp.where(valid[:, None], node_low[served_rows], jnp.zeros((), jnp.bfloat16))
    arrived = lax.all_to_all(
        outgoing.reshape(devices, capacity, LATENT), "dev", split_axis=0, concat_axis=0, tiled=True
    ).reshape(-1, LATENT)
    gathered = arrived[position].reshape(edge.shape[0], 2 * LATENT)
    edge_in = jnp.concatenate([edge.astype(jnp.bfloat16), gathered], axis=1)
    edge_out, edge_kept = mlp_forward(edge_params, edge_in)
    edge_new = edge + edge_out
    buffer = (
        jnp.zeros((devices * capacity, LATENT), jnp.bfloat16)
        .at[recv_pos]
        .set(edge_new.astype(jnp.bfloat16))
    )
    landed = lax.all_to_all(
        buffer.reshape(devices, capacity, LATENT), "dev", split_axis=0, concat_axis=0, tiled=True
    ).reshape(-1, LATENT)
    landed = jnp.where(valid[:, None], landed.astype(jnp.float32), 0.0)
    summed = jnp.zeros(node.shape, jnp.float32).at[served_rows].add(landed)
    node_in = jnp.concatenate([node_low, summed.astype(jnp.bfloat16)], axis=1)
    node_out, node_kept = mlp_forward(node_params, node_in)
    return (node + node_out, edge_new, (edge_kept, node_kept))


def layer_backward(edge_params, node_params, kept, grad_node, grad_edge, routes):
    served_rows, valid, position, recv_pos, devices, capacity = routes
    edge_kept, node_kept = kept
    node_source, node_grads = mlp_backward(node_params, node_kept, grad_node, True)
    grad_total = grad_node + node_source[:, :LATENT]
    summed_low = node_source[:, LATENT:].astype(jnp.bfloat16)
    outgoing = jnp.where(valid[:, None], summed_low[served_rows], jnp.zeros((), jnp.bfloat16))
    returned = lax.all_to_all(
        outgoing.reshape(devices, capacity, LATENT), "dev", split_axis=0, concat_axis=0, tiled=True
    ).reshape(-1, LATENT)
    edge_total = grad_edge + returned[recv_pos].astype(jnp.float32)
    edge_source, edge_grads = mlp_backward(edge_params, edge_kept, edge_total, True)
    edge_prev = edge_total + edge_source[:, :LATENT]
    gathered_low = edge_source[:, LATENT:].reshape(-1, LATENT).astype(jnp.bfloat16)
    buffer = jnp.zeros((devices * capacity, LATENT), jnp.bfloat16).at[position].set(gathered_low)
    landed = lax.all_to_all(
        buffer.reshape(devices, capacity, LATENT), "dev", split_axis=0, concat_axis=0, tiled=True
    ).reshape(-1, LATENT)
    landed = jnp.where(valid[:, None], landed.astype(jnp.float32), 0.0)
    grad_total = grad_total.at[served_rows].add(landed)
    return (grad_total, edge_prev, edge_grads, node_grads)


def local(
    inputs,
    targets,
    geometry,
    land_sea,
    level_mask,
    edge_owners,
    edge_local,
    step_count,
    master,
    first_moment,
    second_moment,
    ema,
):
    segments, total = layout(LATENT, VARS, GEO, LAYERS)
    full_weights = lax.all_gather(master.astype(jnp.bfloat16), "dev", axis=0, tiled=True)
    blocks = unpack(full_weights, segments)
    routes = make_routes(edge_owners, edge_local)
    node, enc_kept = mlp_forward(blocks[0], inputs)
    edge, geo_kept = mlp_forward(blocks[1], geometry)
    layer_kept = []
    for k in range(LAYERS):
        node, edge, kept = layer_forward(blocks[2 + 2 * k], blocks[3 + 2 * k], node, edge, routes)
        layer_kept.append(kept)
    decoded, dec_kept = mlp_forward(blocks[2 + 2 * LAYERS], node.astype(jnp.bfloat16))
    pred = inputs.astype(jnp.float32) + decoded
    ocean = (jnp.arange(VARS) < SEA_VARS).astype(jnp.float32)
    mask = level_mask.astype(jnp.float32) * (
        1.0 - land_sea.astype(jnp.float32)[:, None] * ocean[None, :]
    )
    residual = pred - targets
    error_sum, count = lax.psum((jnp.sum(mask * residual * residual), jnp.sum(mask)), "dev")
    divisor = jnp.maximum(count, 1.0)
    loss = error_sum / divisor
    grad_pred = 2.0 * mask * residual / divisor
    grads = [None] * (3 + 2 * LAYERS)
    dec_source, grads[2 + 2 * LAYERS] = mlp_backward(
        blocks[2 + 2 * LAYERS], dec_kept, grad_pred, True
    )
    grad_node = dec_source
    grad_edge = jnp.zeros(edge.shape, jnp.float32)
    for k in reversed(range(LAYERS)):
        grad_node, grad_edge, grads[2 + 2 * k], grads[3 + 2 * k] = layer_backward(
            blocks[2 + 2 * k], blocks[3 + 2 * k], layer_kept[k], grad_node, grad_edge, routes
        )
    unused, grads[1] = mlp_backward(blocks[1], geo_kept, grad_edge, False)
    unused, grads[0] = mlp_backward(blocks[0], enc_kept, grad_node, False)
    pieces = [
        grads[block_id][part_name].reshape(-1)
        for block_id, part_name, part_shape, offset, entries in segments
    ]
    pieces.append(jnp.zeros((PARAMS - total,), jnp.float32))
    flat_grad = jnp.concatenate(pieces)
    summed_grad = lax.psum(flat_grad, "dev")
    share = master.shape[0]
    own_grad = lax.dynamic_slice_in_dim(summed_grad, lax.axis_index("dev") * share, share)
    squares = jnp.sum(summed_grad * summed_grad)
    grad_norm = jnp.sqrt(squares)
    clipped = own_grad * jnp.minimum(1.0, clip_limit / grad_norm)
    step = step_count[0].astype(jnp.float32)
    new_first = beta_one * first_moment + (1.0 - beta_one) * clipped
    new_second = beta_two * second_moment + (1.0 - beta_two) * clipped * clipped
    first_hat = new_first / (1.0 - beta_one**step)
    second_hat = new_second / (1.0 - beta_two**step)
    new_master = master - learn_rate * (
        first_hat / (jnp.sqrt(second_hat) + adam_eps) + decay_rate * master
    )
    new_ema = ema_keep * ema + (1.0 - ema_keep) * new_master
    return (new_master, new_first, new_second, new_ema, loss, grad_norm)


def solution(mesh):
    in_specs = (
        P("dev", None),
        P("dev", None),
        P("dev", None),
        P("dev"),
        P("dev", None),
        P("dev", None),
        P("dev", None),
        P(),
        P("dev"),
        P("dev"),
        P("dev"),
        P("dev"),
    )
    out_specs = (P("dev"), P("dev"), P("dev"), P("dev"), P(), P())
    return jax.shard_map(local, mesh=mesh, in_specs=in_specs, out_specs=out_specs, check_vma=False)
```

profile of v0, /device:TPU:0, one launch (start us, length us, event | category | flops | bytes accessed | tf_op | source)
XLA Modules:
  0.0 1851.5 jit_solution(10392052022695157452)
XLA Ops:
  8.4 5.4 reshape.886
  21.7 7.6 all-to-all-start
  30.6 5.8 all-to-all-done
  37.6 138.8 %all-gather.3.cloned.1.call-done = bf16[32,1,204544]{2,1,0:T(2,128)(2,1)} async-done(((bf16[1,1,204544]{2,1,0:T(2,128)(2,1)}), bf16[32,1,204544]{2,1,0:T(2,128)(2,1)}) %all-gather.3.cloned.1.call-update) | async-done | bytes 13090832 | tf_op jit(solution)/shard_map/all_gather | solution.py:187
  176.4 277.2 %reduce = bf16[32,204544]{1,0:T(8,128)(2,1)} reduce(bf16[32,1,204544]{2,1,0:T(2,128)(2,1)} %all-gather.3.cloned.1.call-done, bf16[]{:T(256)} %constant.119), dimensions={1}, to_apply=%all-gather.reduce_sub_computation | reduce | bytes 26181634 | tf_op jit(solution)/shard_map/all_gather | solution.py:187
  453.6 23.7 %reshape.887 = bf16[6545408]{0:T(1024)(128)(2,1)} reshape(bf16[32,204544]{1,0:T(8,128)(2,1)} %reduce) | data formatting | bytes 26181632
  481.3 5.1 fusion.104
  520.1 16.8 all-to-all-done.1
  558.8 12.6 all-to-all-done.2
  571.6 10.2 scatter_custom_fusion.2
  581.7 4.8 copy.80
  586.6 6.7 multiply_convert_fusion.12
  599.7 4.3 fusion.100
  618.2 17.0 all-to-all-done.3
  653.0 18.0 all-to-all-done.4
  671.2 10.1 scatter_custom_fusion.4
  681.2 4.8 copy.82
  686.1 6.8 multiply_convert_fusion.11
  716.1 17.3 all-to-all-done.5
  754.6 14.6 all-to-all-done.6
  770.5 10.5 scatter_custom_fusion.6
  781.0 4.8 copy.84
  785.8 6.9 multiply_convert_fusion.10
  808.9 39.5 %all-reduce = (f32[]{:T(128)}, f32[]{:T(128)}) all-reduce(f32[]{:T(128)} %get-tuple-element.19, f32[]{:T(128)} %get-tuple-element.18), channel_id=1, replica_groups=mesh['dev'=32] {'dev'}, use_global_device_ids=true, to_apply=%region_27.28 | all-reduce | flops 2 | bytes 16 | tf_op jit(solution)/shard_map/psum | solution.py:203
  859.4 5.4 copy.85
  864.8 5.5 multiply_reduce_fusion.1
  890.4 4.5 all-to-all-start.7
  898.8 16.7 all-to-all-done.7
  935.8 4.7 fusion.18
  951.1 12.4 scatter_custom_fusion.8
  963.6 5.4 copy.86
  969.0 5.0 multiply_reduce_fusion.2
  1010.0 6.0 all-to-all-done.9
  1035.2 5.0 fusion.107
  1044.9 6.0 all-to-all-done.10
  1051.0 12.3 scatter_custom_fusion.10
  1063.3 5.4 copy.87
  1068.8 4.9 multiply_reduce_fusion.3
  1097.8 4.6 fusion.16
  1107.9 5.0 fusion.108
  1112.9 5.5 all-to-all-done.11
  1141.4 12.1 all-to-all-done.12
  1153.6 12.2 scatter_custom_fusion.12
  1168.4 5.4 copy.88
  1173.8 5.0 multiply_reduce_fusion.4
  1191.5 231.7 %concatenate.27 = f32[6545408]{0:T(1024)} concatenate(f32[116224]{0:T(1024)} %reshape.644, f32[512]{0:T(512)S(1)} %get-tuple-element.150, f32[262144]{0:T(1024)} %bitcast.184, f32[512]{0:T(512)S(1)} %get-tuple-element.59, f32[512]{0:T(512)S(1)} %get-tuple-element.12, f32[512]{0:T(512)S(1)} %reduce_sum.668, f32[2048]{0:T(1024)S(1)} %bitcast.185, f32[512]{0:T(512)S(1)} %get-tuple-element.152, ...), dimensions={0} | concatenate | bytes 52363264 | tf_op jit(solution)/shard_map/concatenate | solution.py:224
  1424.7 402.6 %all-reduce.3.cloned.1.call-done = f32[6545408]{0:T(1024)} async-done(((f32[6545408]{0:T(1024)}), f32[6545408]{0:T(1024)}) %all-reduce.3.cloned.1.call-update) | async-done | bytes 26181648 | tf_op jit(solution)/shard_map/psum | solution.py:225
  1827.3 10.4 multiply_reduce_fusion
  (700 shorter events, 365.8 us)
Async XLA Ops:
  7.2 509.1 %copy-start = (bf16[256,4]{0,1:T(4,128)(2,1)S(1)}, bf16[256,4]{0,1:T(4,128)(2,1)}, u32[]{:S(2)}) copy-start(bf16[256,4]{0,1:T(4,128)(2,1)} %param.14) | copy-start | bytes 6148
  7.2 169.3 %all-gather.3.cloned.1.call-start = ((), (), s32[]{:S(2)}) async-start(), calls=%async_computation.14 | async-start | bytes 26999808 | tf_op jit(solution)/shard_map/all_gather | solution.py:187
  18.5 12.1 copy-start.174
  21.7 14.7 all-to-all-start
  37.6 416.1 %copy-start.169 = (s32[640]{0:T(1024)}, s32[640]{0:T(1024)S(1)}, u32[]{:S(2)}) copy-start(s32[640]{0:T(1024)S(1)} %reshape.782) | copy-start | bytes 7684
  37.6 471.9 %copy-start.118 = (s32[1024]{0:T(1024)}, s32[1024]{0:T(1024)S(1)}, u32[]{:S(2)}) copy-start(s32[1024]{0:T(1024)S(1)} %pad_clamp_fusion.2) | copy-start | bytes 12292
  479.5 18.2 copy-start.187
  479.5 23.6 %copy-start.122 = (f32[512]{0:T(512)}, f32[512]{0:T(512)S(1)}, u32[]{:S(2)}) copy-start(f32[512]{0:T(512)S(1)} %get-tuple-element.115) | copy-start | bytes 6148
  479.5 23.6 %copy-start.130 = (f32[512]{0:T(512)}, f32[512]{0:T(512)S(1)}, u32[]{:S(2)}) copy-start(f32[512]{0:T(512)S(1)} %get-tuple-element.114) | copy-start | bytes 6148
  479.5 23.6 %copy-start.163 = (f32[512]{0:T(512)}, f32[512]{0:T(512)S(1)}, u32[]{:S(2)}) copy-start(f32[512]{0:T(512)S(1)} %get-tuple-element.113) | copy-start | bytes 6148
  502.4 94.3 %copy-start.106 = (f32[2048]{0:T(1024)}, f32[2048]{0:T(1024)S(1)}, u32[]{:S(2)}) copy-start(f32[2048]{0:T(1024)S(1)} %broadcast_multiply_fusion.11) | copy-start | bytes 24580
  513.5 23.4 %all-to-all-start.1 = ((bf16[32,20,512]{2,1,0:T(8,128)(2,1)}), bf16[32,20,512]{2,1,0:T(8,128)(2,1)S(1)}, u32[]{:S(2)}, u32[]{:S(2)}) async-start(bf16[32,20,512]{2,1,0:T(8,128)(2,1)} %broadcast_select_fusion.5), calls=%async_computation.1 | async-start | bytes 1572864 | tf_op jit(solution)/shard_map/all_to_all | solution.py:127
  517.7 25.1 %copy-start.20 = (f32[256,512]{1,0:T(8,128)}, f32[256,512]{1,0:T(8,128)S(1)}, u32[]{:S(2)}) copy-start(f32[256,512]{1,0:T(8,128)S(1)} %get-tuple-element.128) | copy-start | bytes 1572868
  517.8 21.8 %copy-start.34 = (bf16[1536,512]{1,0:T(8,128)(2,1)S(1)}, bf16[1536,512]{1,0:T(8,128)(2,1)}, u32[]{:S(2)}) copy-start(bf16[1536,512]{1,0:T(8,128)(2,1)} %slice.397) | copy-start | bytes 4718596
  543.9 95.5 %copy-start.73 = (bf16[256,512]{1,0:T(8,128)(2,1)}, bf16[256,512]{1,0:T(8,128)(2,1)S(1)}, u32[]{:S(2)}) copy-start(bf16[256,512]{1,0:T(8,128)(2,1)S(1)} %get-tuple-element.65) | copy-start | bytes 786436
  546.8 24.6 %all-to-all-start.2 = ((bf16[32,20,512]{2,1,0:T(8,128)(2,1)}), bf16[32,20,512]{2,1,0:T(8,128)(2,1)S(1)}, u32[]{:S(2)}, u32[]{:S(2)}) async-start(bf16[32,20,512]{2,1,0:T(8,128)(2,1)} %reshape.630), calls=%async_computation.2 | async-start | bytes 1572864 | tf_op jit(solution)/shard_map/all_to_all | solution.py:139
  554.8 16.8 copy-start.137
  558.8 37.9 %copy-start.148 = (f32[512]{0:T(512)}, f32[512]{0:T(512)S(1)}, u32[]{:S(2)}) copy-start(f32[512]{0:T(512)S(1)} %get-tuple-element.87) | copy-start | bytes 6148
  609.8 26.7 %copy-start.158 = (s32[1024]{0:T(1024)S(1)}, s32[1024]{0:T(1024)}, u32[]{:S(2)}) copy-start(s32[1024]{0:T(1024)} %pad_clamp_fusion.1) | copy-start | bytes 12292
  610.9 24.4 %all-to-all-start.3 = ((bf16[32,20,512]{2,1,0:T(8,128)(2,1)}), bf16[32,20,512]{2,1,0:T(8,128)(2,1)}, u32[]{:S(2)}, u32[]{:S(2)}) async-start(bf16[32,20,512]{2,1,0:T(8,128)(2,1)} %broadcast_select_fusion.4), calls=%async_computation.3 | async-start | bytes 1572864 | tf_op jit(solution)/shard_map/all_to_all | solution.py:127
  615.6 25.5 %copy-start.36 = (bf16[1536,512]{1,0:T(8,128)(2,1)}, bf16[1536,512]{1,0:T(8,128)(2,1)S(1)}, u32[]{:S(2)}) copy-start(bf16[1536,512]{1,0:T(8,128)(2,1)S(1)} %slice.413) | copy-start | bytes 4718596
  645.8 25.4 %copy-start.138 = (pred[640]{0:T(1024)(128)(4,1)S(1)}, pred[640]{0:T(1024)(128)(4,1)}, u32[]{:S(2)}) copy-start(pred[640]{0:T(1024)(128)(4,1)} %gt.15) | copy-start | bytes 1924
  646.8 24.2 %all-to-all-start.4 = ((bf16[32,20,512]{2,1,0:T(8,128)(2,1)}), bf16[32,20,512]{2,1,0:T(8,128)(2,1)S(1)}, u32[]{:S(2)}, u32[]{:S(2)}) async-start(bf16[32,20,512]{2,1,0:T(8,128)(2,1)} %reshape.633), calls=%async_computation.4 | async-start | bytes 1572864 | tf_op jit(solution)/shard_map/all_to_all | solution.py:139
  708.0 25.5 %copy-start.159 = (s32[1024]{0:T(1024)S(1)}, s32[1024]{0:T(1024)}, u32[]{:S(2)}) copy-start(s32[1024]{0:T(1024)} %pad_clamp_fusion.1) | copy-start | bytes 12292
  709.1 24.2 %all-to-all-start.5 = ((bf16[32,20,512]{2,1,0:T(8,128)(2,1)}), bf16[32,20,512]{2,1,0:T(8,128)(2,1)S(1)}, u32[]{:S(2)}, u32[]{:S(2)}) async-start(bf16[32,20,512]{2,1,0:T(8,128)(2,1)} %broadcast_select_fusion.3), calls=%async_computation.5 | async-start | bytes 1572864 | tf_op jit(solution)/shard_map/all_to_all | solution.py:127
  716.1 19.7 %copy-start.76 = (bf16[256,512]{1,0:T(8,128)(2,1)S(1)}, bf16[256,512]{1,0:T(8,128)(2,1)}, u32[]{:S(2)}) copy-start(bf16[256,512]{1,0:T(8,128)(2,1)} %copy-done.75) | copy-start | bytes 786436
  716.1 19.7 %copy-start.186 = (f32[512]{0:T(512)S(1)}, f32[512]{0:T(512)}, u32[]{:S(2)}) copy-start(f32[512]{0:T(512)} %get-tuple-element.77) | copy-start | bytes 6148
  738.0 12.3 copy-start.48
  740.0 12.8 copy-start.53
  744.9 25.6 %copy-start.139 = (pred[640]{0:T(1024)(128)(4,1)S(1)}, pred[640]{0:T(1024)(128)(4,1)}, u32[]{:S(2)}) copy-start(pred[640]{0:T(1024)(128)(4,1)} %gt.15) | copy-start | bytes 1924
  744.9 24.4 %all-to-all-start.6 = ((bf16[32,20,512]{2,1,0:T(8,128)(2,1)}), bf16[32,20,512]{2,1,0:T(8,128)(2,1)}, u32[]{:S(2)}, u32[]{:S(2)}) async-start(bf16[32,20,512]{2,1,0:T(8,128)(2,1)} %reshape.636), calls=%async_computation.6 | async-start | bytes 1572864 | tf_op jit(solution)/shard_map/all_to_all | solution.py:139
  890.4 25.2 %all-to-all-start.7 = ((bf16[32,20,512]{2,1,0:T(8,128)(2,1)}), bf16[32,20,512]{2,1,0:T(8,128)(2,1)}, u32[]{:S(2)}, u32[]{:S(2)}) async-start(bf16[32,20,512]{2,1,0:T(8,128)(2,1)} %broadcast_select_fusion.2), calls=%async_computation.7 | async-start | bytes 1572864 | tf_op jit(solution)/shard_map/all_to_all | solution.py:156
  898.8 19.7 %copy-start.103 = (bf16[512,512]{1,0:T(8,128)(2,1)S(1)}, bf16[512,512]{1,0:T(8,128)(2,1)}, u32[]{:S(2)}) copy-start(bf16[512,512]{1,0:T(8,128)(2,1)} %slice.432) | copy-start | bytes 1572868
  898.8 19.7 %copy-start.201 = (f32[256,512]{1,0:T(8,128)S(1)}, f32[256,512]{1,0:T(8,128)}, u32[]{:S(2)}) copy-start(f32[256,512]{1,0:T(8,128)} %copy-done.200) | copy-start | bytes 1572868
  925.5 24.4 %all-to-all-start.8 = ((bf16[32,20,512]{2,1,0:T(8,128)(2,1)}), bf16[32,20,512]{2,1,0:T(8,128)(2,1)}, u32[]{:S(2)}, u32[]{:S(2)}) async-start(bf16[32,20,512]{2,1,0:T(8,128)(2,1)} %reshape.639), calls=%async_computation.8 | async-start | bytes 1572864 | tf_op jit(solution)/shard_map/all_to_all | solution.py:164
  991.7 24.4 %all-to-all-start.9 = ((bf16[32,20,512]{2,1,0:T(8,128)(2,1)}), bf16[32,20,512]{2,1,0:T(8,128)(2,1)S(1)}, u32[]{:S(2)}, u32[]{:S(2)}) async-start(bf16[32,20,512]{2,1,0:T(8,128)(2,1)} %broadcast_select_fusion.1), calls=%async_computation.9 | async-start | bytes 1572864 | tf_op jit(solution)/shard_map/all_to_all | solution.py:156
  1026.4 24.4 %all-to-all-start.10 = ((bf16[32,20,512]{2,1,0:T(8,128)(2,1)}), bf16[32,20,512]{2,1,0:T(8,128)(2,1)S(1)}, u32[]{:S(2)}, u32[]{:S(2)}) async-start(bf16[32,20,512]{2,1,0:T(8,128)(2,1)} %reshape.641), calls=%async_computation.10 | async-start | bytes 1572864 | tf_op jit(solution)/shard_map/all_to_all | solution.py:164
  1093.5 24.8 %all-to-all-start.11 = ((bf16[32,20,512]{2,1,0:T(8,128)(2,1)}), bf16[32,20,512]{2,1,0:T(8,128)(2,1)}, u32[]{:S(2)}, u32[]{:S(2)}) async-start(bf16[32,20,512]{2,1,0:T(8,128)(2,1)} %broadcast_select_fusion), calls=%async_computation.11 | async-start | bytes 1572864 | tf_op jit(solution)/shard_map/all_to_all | solution.py:156
  1107.9 12.9 copy-start.26
  1107.9 12.9 copy-start.147
  1107.9 12.9 copy-start.157
  1107.9 12.9 copy-start.167
  1129.2 24.3 %all-to-all-start.12 = ((bf16[32,20,512]{2,1,0:T(8,128)(2,1)}), bf16[32,20,512]{2,1,0:T(8,128)(2,1)S(1)}, u32[]{:S(2)}, u32[]{:S(2)}) async-start(bf16[32,20,512]{2,1,0:T(8,128)(2,1)} %reshape.643), calls=%async_computation.12 | async-start | bytes 1572864 | tf_op jit(solution)/shard_map/all_to_all | solution.py:164
  1132.8 694.5 %all-reduce.3.cloned.1.call-start = ((), (), s32[]{:S(2)}) async-start(), calls=%async_computation.13 | async-start | bytes 52363264 | tf_op jit(solution)/shard_map/psum | solution.py:225
  1424.6 413.8 %copy-start.50 = (f32[204544]{0:T(1024)S(1)}, f32[204544]{0:T(1024)}, u32[]{:S(2)}) copy-start(f32[204544]{0:T(1024)} %param.20) | copy-start | bytes 2454532
  1424.6 413.8 %copy-start.88 = (f32[204544]{0:T(1024)S(1)}, f32[204544]{0:T(1024)}, u32[]{:S(2)}) copy-start(f32[204544]{0:T(1024)} %param.23) | copy-start | bytes 2454532
  1424.7 413.8 %copy-start.89 = (f32[204544]{0:T(1024)S(1)}, f32[204544]{0:T(1024)}, u32[]{:S(2)}) copy-start(f32[204544]{0:T(1024)} %param.22) | copy-start | bytes 2454532
  1424.7 413.8 %copy-start.90 = (f32[204544]{0:T(1024)S(1)}, f32[204544]{0:T(1024)}, u32[]{:S(2)}) copy-start(f32[204544]{0:T(1024)} %param.21) | copy-start | bytes 2454532
  (183 other events, 738.1 us)
Sparse Core Ops, SparseCore 0:
  14.0 162.4 all-gather.2
  1423.4 403.9 all-reduce.2
where the time goes:
time: 1870 us; the launch traced here: 1850 us
  waiting for transfers between devices  693 us (37%)
  local copies, waits for them, and re-layouts  482 us (26%)
  other arithmetic  449 us (24%)
  matrix products  112 us (6%)
  starting transfers between devices  53.1 us (3%)
  blocking collectives  39.5 us (2%)
  between operations  22.6 us (1%)
    psum x1, waiting for transfers between devices, local(): summed_grad = lax.psum(flat_grad, 'dev')  403 us
    all_gather x1, other arithmetic, local(): lax.all_gather(master.astype(jnp.bfloat16), 'dev', axis=0, tiled=True)  277 us
    concatenate x1, local copies, waits for them, and re-layouts, local(): flat_grad = jnp.concatenate(pieces)  232 us
    all_gather x1, waiting for transfers between devices, local(): lax.all_gather(master.astype(jnp.bfloat16), 'dev', axis=0, tiled=True)  139 us
    unnamed x451, local copies, waits for them, and re-layouts  92.5 us
    all_to_all x3, waiting for transfers between devices, layer_forward(): lax.all_to_all(outgoing.reshape(devices, capacity, LATENT), 'dev', split_...  51.1 us
    all_to_all x3, waiting for transfers between devices, layer_forward(): lax.all_to_all(buffer.reshape(devices, capacity, LATENT), 'dev', split_ax...  45.3 us
    psum x1, blocking collectives, local(): lax.psum((jnp.sum(mask * residual * residual), jnp.sum(mask)), 'dev')  39.5 us
  transfers between devices with their start and end apart: 15, of which 15 were waited for; matrix products, arithmetic and copies ran while one was open for 6% of the time, Pallas kernels for 0%

commit v1 on v0

--- a/solution.py
+++ b/solution.py
@@ -222,7 +222,13 @@
     ]
     pieces.append(jnp.zeros((PARAMS - total,), jnp.float32))
     flat_grad = jnp.concatenate(pieces)
-    summed_grad = lax.psum(flat_grad, "dev")
+    peers = lax.axis_size("dev")
+    summed_grad, reach = (flat_grad, 1)
+    while reach < peers:
+        summed_grad = summed_grad + lax.ppermute(
+            summed_grad, "dev", [(i, i ^ reach) for i in range(peers)]
+        )
+        reach = 2 * reach
     share = master.shape[0]
     own_grad = lax.dynamic_slice_in_dim(summed_grad, lax.axis_index("dev") * share, share)
     squares = jnp.sum(summed_grad * summed_grad)

time: 1870 us -> 4440 us (2.37)
  waiting for transfers between devices: 693 us -> 3130 us
  other arithmetic: 449 us -> 572 us
    ppermute x0 -> x5, waiting for transfers between devices: none -> 2840 us  [local(): lax.ppermute(summed_grad, 'dev', [(i, i ^ reach) for i in range(peers)])]
    psum x1 -> x0, waiting for transfers between devices: 403 us -> none  [local(): summed_grad = lax.psum(flat_grad, 'dev')]
    add x0 -> x4, other arithmetic: none -> 106 us  [local(): summed_grad + lax.ppermute(summed_grad, 'dev', [(i, i ^ reach) for i in r...]
  transfers between devices with their start and end apart: 15 -> 19, of which waited for: 15 -> 19; matrix products, arithmetic and copies ran while one was open for 6% -> 2% of each run, Pallas kernels for 0% -> 0%
where the time goes in v1:
time: 4440 us; the launch traced here: 4420 us
  waiting for transfers between devices  3130 us (70%)
  other arithmetic  572 us (13%)
  local copies, waits for them, and re-layouts  481 us (11%)
  matrix products  112 us (3%)
  starting transfers between devices  59.6 us (1%)
    ppermute x5, waiting for transfers between devices, local(): lax.ppermute(summed_grad, 'dev', [(i, i ^ reach) for i in range(peers)])  2840 us
    all_gather x1, other arithmetic, local(): lax.all_gather(master.astype(jnp.bfloat16), 'dev', axis=0, tiled=True)  277 us
    concatenate x1, local copies, waits for them, and re-layouts, local(): flat_grad = jnp.concatenate(pieces)  232 us
    all_gather x1, waiting for transfers between devices, local(): lax.all_gather(master.astype(jnp.bfloat16), 'dev', axis=0, tiled=True)  139 us
    add x4, other arithmetic, local(): summed_grad + lax.ppermute(summed_grad, 'dev', [(i, i ^ reach) for i in r...  106 us
    unnamed x451, local copies, waits for them, and re-layouts  91.3 us
  transfers between devices with their start and end apart: 19, of which 19 were waited for; matrix products, arithmetic and copies ran while one was open for 2% of the time, Pallas kernels for 0%

profile of v1, /device:TPU:0, one launch (start us, length us, event | category | flops | bytes accessed | tf_op | source)
XLA Modules:
  0.0 4422.0 jit_solution(17384175065957021259)
XLA Ops:
  8.4 5.4 reshape.886
  21.7 7.6 all-to-all-start
  30.6 5.7 all-to-all-done
  37.6 138.8 %all-gather.3.cloned.1.call-done = bf16[32,1,204544]{2,1,0:T(2,128)(2,1)} async-done(((bf16[1,1,204544]{2,1,0:T(2,128)(2,1)}), bf16[32,1,204544]{2,1,0:T(2,128)(2,1)}) %all-gather.3.cloned.1.call-update) | async-done | bytes 13090832 | tf_op jit(solution)/shard_map/all_gather | solution.py:187
  176.4 277.2 %reduce = bf16[32,204544]{1,0:T(8,128)(2,1)} reduce(bf16[32,1,204544]{2,1,0:T(2,128)(2,1)} %all-gather.3.cloned.1.call-done, bf16[]{:T(256)} %constant.119), dimensions={1}, to_apply=%all-gather.reduce_sub_computation | reduce | bytes 26181634 | tf_op jit(solution)/shard_map/all_gather | solution.py:187
  453.7 23.7 reshape.887
  481.3 5.1 fusion.104
  520.1 16.8 all-to-all-done.1
  558.9 12.6 all-to-all-done.2
  571.6 10.1 scatter_custom_fusion.2
  586.6 6.6 multiply_convert_fusion.12
  616.9 17.0 all-to-all-done.3
  651.7 18.0 all-to-all-done.4
  669.9 10.1 scatter_custom_fusion.4
  684.8 6.8 multiply_convert_fusion.11
  714.8 17.3 all-to-all-done.5
  753.3 14.6 all-to-all-done.6
  769.2 10.5 scatter_custom_fusion.6
  784.5 6.8 multiply_convert_fusion.10
  807.6 39.5 all-reduce
  858.2 5.4 copy.85
  863.6 5.5 multiply_reduce_fusion.1
  897.6 16.7 all-to-all-done.7
  949.9 12.5 scatter_custom_fusion.8
  962.4 5.4 copy.86
  967.8 5.0 multiply_reduce_fusion.2
  1008.9 6.0 all-to-all-done.9
  1034.0 5.1 fusion.107
  1043.8 5.9 all-to-all-done.10
  1049.8 12.3 scatter_custom_fusion.10
  1062.2 5.4 copy.87
  1106.8 5.1 fusion.108
  1111.8 5.4 all-to-all-done.11
  1140.3 12.2 all-to-all-done.12
  1152.6 12.3 scatter_custom_fusion.12
  1167.5 5.4 copy.88
  1172.9 5.1 multiply_reduce_fusion.4
  1190.6 231.6 %concatenate.27 = f32[6545408]{0:T(1024)} concatenate(f32[116224]{0:T(1024)} %reshape.644, f32[512]{0:T(512)S(1)} %get-tuple-element.152, f32[262144]{0:T(1024)} %bitcast.184, f32[512]{0:T(512)S(1)} %get-tuple-element.61, f32[512]{0:T(512)S(1)} %get-tuple-element.12, f32[512]{0:T(512)S(1)} %reduce_sum.668, f32[2048]{0:T(1024)S(1)} %bitcast.185, f32[512]{0:T(512)S(1)} %get-tuple-element.154, ...), dimensions={0} | concatenate | bytes 52363264 | tf_op jit(solution)/shard_map/concatenate | solution.py:224
  1422.3 38.9 collective-permute-done
  1461.2 26.5 add.603
  1489.2 562.6 %collective-permute-done.1 = f32[6545408]{0:T(1024)} collective-permute-done((f32[6545408]{0:T(1024)}, f32[6545408]{0:T(1024)}, u32[]{:S(2)}, u32[]{:S(2)}) %collective-permute-start.1) | collective-permute-done | bytes 26181664 | tf_op jit(solution)/shard_map/ppermute | solution.py:228
  2051.8 26.5 add.604
  2079.8 561.8 %collective-permute-done.2 = f32[6545408]{0:T(1024)} collective-permute-done((f32[6545408]{0:T(1024)}, f32[6545408]{0:T(1024)}, u32[]{:S(2)}, u32[]{:S(2)}) %collective-permute-start.2) | collective-permute-done | bytes 26181664 | tf_op jit(solution)/shard_map/ppermute | solution.py:228
  2641.6 26.5 add.605
  2669.5 561.0 %collective-permute-done.3 = f32[6545408]{0:T(1024)} collective-permute-done((f32[6545408]{0:T(1024)}, f32[6545408]{0:T(1024)}, u32[]{:S(2)}, u32[]{:S(2)}) %collective-permute-start.3) | collective-permute-done | bytes 26181664 | tf_op jit(solution)/shard_map/ppermute | solution.py:228
  3230.4 26.5 add.606
  3260.4 1119.9 %collective-permute-done.4 = f32[6545408]{0:T(1024)} collective-permute-done((f32[6545408]{0:T(1024)}, f32[6545408]{0:T(1024)}, u32[]{:S(2)}, u32[]{:S(2)}) %collective-permute-start.4) | collective-permute-done | bytes 26181664 | tf_op jit(solution)/shard_map/ppermute | solution.py:228
  4380.3 27.8 multiply_reduce_fusion
  (711 shorter events, 408.7 us)
Async XLA Ops:
  7.2 509.1 %copy-start = (bf16[256,4]{0,1:T(4,128)(2,1)S(1)}, bf16[256,4]{0,1:T(4,128)(2,1)}, u32[]{:S(2)}) copy-start(bf16[256,4]{0,1:T(4,128)(2,1)} %param.14) | copy-start | bytes 6148
  7.2 169.3 %all-gather.3.cloned.1.call-start = ((), (), s32[]{:S(2)}) async-start(), calls=%async_computation.13 | async-start | bytes 26999808 | tf_op jit(solution)/shard_map/all_gather | solution.py:187
  21.7 14.7 all-to-all-start
  37.6 416.1 %copy-start.169 = (s32[640]{0:T(1024)}, s32[640]{0:T(1024)S(1)}, u32[]{:S(2)}) copy-start(s32[640]{0:T(1024)S(1)} %reshape.782) | copy-start | bytes 7684
  37.6 471.9 %copy-start.118 = (s32[1024]{0:T(1024)}, s32[1024]{0:T(1024)S(1)}, u32[]{:S(2)}) copy-start(s32[1024]{0:T(1024)S(1)} %pad_clamp_fusion.2) | copy-start | bytes 12292
  479.5 18.1 copy-start.187
  479.5 23.5 copy-start.122
  479.5 23.5 copy-start.130
  479.5 23.5 copy-start.163
  502.4 93.0 %copy-start.106 = (f32[2048]{0:T(1024)}, f32[2048]{0:T(1024)S(1)}, u32[]{:S(2)}) copy-start(f32[2048]{0:T(1024)S(1)} %broadcast_multiply_fusion.11) | copy-start | bytes 24580
  513.5 23.4 all-to-all-start.1
  517.7 25.1 copy-start.20
  517.8 21.8 copy-start.34
  543.9 94.3 %copy-start.73 = (bf16[256,512]{1,0:T(8,128)(2,1)}, bf16[256,512]{1,0:T(8,128)(2,1)S(1)}, u32[]{:S(2)}) copy-start(bf16[256,512]{1,0:T(8,128)(2,1)S(1)} %get-tuple-element.67) | copy-start | bytes 786436
  546.8 24.6 all-to-all-start.2
  554.8 16.8 copy-start.137
  558.9 36.5 copy-start.148
  608.5 26.7 copy-start.158
  609.6 24.4 all-to-all-start.3
  614.3 25.5 copy-start.36
  644.5 25.4 copy-start.138
  645.5 24.2 all-to-all-start.4
  706.8 25.4 copy-start.159
  707.8 24.2 all-to-all-start.5
  714.8 19.7 copy-start.76
  714.8 19.7 copy-start.186
  743.6 25.6 copy-start.139
  743.6 24.4 all-to-all-start.6
  889.2 25.2 all-to-all-start.7
  897.6 19.7 copy-start.103
  897.6 19.7 copy-start.201
  924.3 24.4 all-to-all-start.8
  990.5 24.4 all-to-all-start.9
  1025.2 24.5 all-to-all-start.10
  1092.4 24.8 all-to-all-start.11
  1106.7 12.9 copy-start.147
  1106.7 12.9 copy-start.157
  1106.7 12.9 copy-start.167
  1128.1 24.4 all-to-all-start.12
  1422.3 38.9 collective-permute-start
  1487.7 564.1 %collective-permute-start.1 = (f32[6545408]{0:T(1024)}, f32[6545408]{0:T(1024)}, u32[]{:S(2)}, u32[]{:S(2)}) collective-permute-start(f32[6545408]{0:T(1024)} %add.603), channel_id=1, source_target_pairs={{0,2},{1,3},{2,0},{3,1},{4,6},{5,7},{6,4},{7,5},{8,10},{9,11},{10,... | collective-permute-start | bytes 78544904 | tf_op jit(solution)/shard_map/ppermute | solution.py:228
  2078.3 563.3 %collective-permute-start.2 = (f32[6545408]{0:T(1024)}, f32[6545408]{0:T(1024)}, u32[]{:S(2)}, u32[]{:S(2)}) collective-permute-start(f32[6545408]{0:T(1024)} %add.604), channel_id=1, source_target_pairs={{0,4},{1,5},{2,6},{3,7},{4,0},{5,1},{6,2},{7,3},{8,12},{9,13},{10,... | collective-permute-start | bytes 78544904 | tf_op jit(solution)/shard_map/ppermute | solution.py:228
  2668.1 562.4 %collective-permute-start.3 = (f32[6545408]{0:T(1024)}, f32[6545408]{0:T(1024)}, u32[]{:S(2)}, u32[]{:S(2)}) collective-permute-start(f32[6545408]{0:T(1024)} %add.605), channel_id=1, source_target_pairs={{0,8},{1,9},{2,10},{3,11},{4,12},{5,13},{6,14},{7,15},{8,0},{9,1},... | collective-permute-start | bytes 78544904 | tf_op jit(solution)/shard_map/ppermute | solution.py:228
  3256.9 1123.4 %collective-permute-start.4 = (f32[6545408]{0:T(1024)}, f32[6545408]{0:T(1024)}, u32[]{:S(2)}, u32[]{:S(2)}) collective-permute-start(f32[6545408]{0:T(1024)} %add.606), channel_id=1, source_target_pairs={{0,16},{1,17},{2,18},{3,19},{4,20},{5,21},{6,22},{7,23},{8,24},{9,... | collective-permute-start | bytes 78544904 | tf_op jit(solution)/shard_map/ppermute | solution.py:228
  3260.4 1148.5 %copy-start.50 = (f32[204544]{0:T(1024)S(1)}, f32[204544]{0:T(1024)}, u32[]{:S(2)}) copy-start(f32[204544]{0:T(1024)} %param.20) | copy-start | bytes 2454532
  3260.4 1148.5 %copy-start.88 = (f32[204544]{0:T(1024)S(1)}, f32[204544]{0:T(1024)}, u32[]{:S(2)}) copy-start(f32[204544]{0:T(1024)} %param.23) | copy-start | bytes 2454532
  3260.4 1148.5 %copy-start.89 = (f32[204544]{0:T(1024)S(1)}, f32[204544]{0:T(1024)}, u32[]{:S(2)}) copy-start(f32[204544]{0:T(1024)} %param.22) | copy-start | bytes 2454532
  3260.4 1148.5 %copy-start.90 = (f32[204544]{0:T(1024)S(1)}, f32[204544]{0:T(1024)}, u32[]{:S(2)}) copy-start(f32[204544]{0:T(1024)} %param.21) | copy-start | bytes 2454532
  (187 other events, 785.8 us)
Sparse Core Ops, SparseCore 0:
  14.0 162.4 all-gather.2
